TPU v7x, 512 devices: a whole 4x8x8 slice. The times are simulated.
512 devices in a mesh: lat: 16 (over y_lo, x, core), lon: 32 (over z, y_hi).
Axes of the slice: x: 4, y: 8 (y_hi: 4, y_lo: 2; y = y_hi * 2 + y_lo), z: 8, core: 2. Of those that a mesh axis runs over, the one named last changes fastest.
Arguments:
- features: float32 [4, 96, 384, 192], P(None, 'lat', 'lon'), may hold values from -460 to 460
- cotangent: float32 [4, 96, 384, 192], P(None, 'lat', 'lon'), may hold values from -6 to 6
- norm_gain: float32 [192], replicated, may hold values from 0.1 to 1.9
- norm_shift: float32 [192], replicated, may hold values from -3 to 3
- qkv_weight: float32 [192, 576], replicated, may hold values from -0.4375 to 0.4375
- out_weight: float32 [192, 192], replicated, may hold values from -0.4375 to 0.4375
- bias_table: float32 [16, 2, 6, 23, 144], P('lat'), may hold values from -6 to 305
Outputs:
- grad_features: float32 [4, 96, 384, 192], P(None, 'lat', 'lon')
- grad_weights: float32 [192, 768], P('lat', 'lon')
- grad_bias: float32 [16, 2, 6, 23, 144], P('lat')
- grad_norm: float32 [2, 192], replicated
All inputs are finite; a program needn't handle non-finite values.
Results may differ from a plain program's by a relative error of at most 0.0003.
Values sent between devices are 32-bit elements; how exact they have to be, the bound alone decides.
A program may use at most 128 MiB of HBM per device.

v0:
```python
import math
import jax
import jax.numpy as jnp
from jax import lax
from jax.sharding import PartitionSpec as P

D = 192
HEADS = 6
HEAD = 32
ZP = 4
WZ = 2
WLAT = 6
WLON = 12
PW = 2
WIN = 144
LONREL = 23
PAIRS = 144
EPSILON = 1e-05
HIGH = lax.Precision.HIGHEST


def passed_along(value, axis, steps):
    count = lax.axis_size(axis)
    pairs = [(source, (source + steps) % count) for source in range(count)]
    return lax.ppermute(value, axis, pairs)


def offset_table():
    columns = jnp.arange(WLON, dtype=jnp.int32)
    offset = columns[None, :] - columns[:, None] + (WLON - 1)
    return (offset[:, :, None] == jnp.arange(LONREL, dtype=jnp.int32)[None, None, :]).astype(
        jnp.float32
    )


def level_valid():
    level = jnp.arange(WIN, dtype=jnp.int32) // (WLAT * WLON)
    same_level = level[:, None] == level[None, :]
    window_index = jnp.arange(PW, dtype=jnp.int32)[:, None, None]
    return (window_index > 0) | same_level[None, :, :]


def shards(features, cotangent, norm_gain, norm_shift, qkv_weight, out_weight, bias_table):
    half_cols = WLON // 2
    lat_blocks = features.shape[1] // WLAT
    lon_blocks = features.shape[2] // WLON
    onehot = offset_table()
    score_scale = HEAD ** (-0.5)
    average = jnp.mean(features, -1, keepdims=True)
    centred = features - average
    inverse = lax.rsqrt(jnp.mean(centred * centred, -1, keepdims=True) + EPSILON)
    standard = centred * inverse
    normed = standard * norm_gain + norm_shift
    lifted = jnp.roll(normed, 1, 0)
    upstream = jnp.roll(cotangent, 1, 0)
    borrowed, borrowed_grad = passed_along(
        (lifted[:, :, -half_cols:], upstream[:, :, -half_cols:]), "lon", 1
    )
    joined = jnp.concatenate([borrowed, lifted[:, :, :-half_cols]], axis=2)
    joined_grad = jnp.concatenate([borrowed_grad, upstream[:, :, :-half_cols]], axis=2)

    def to_windows(grid_block):
        shaped = grid_block.reshape(PW, WZ, lat_blocks, WLAT, lon_blocks, WLON, D)
        return shaped.transpose(0, 2, 4, 1, 3, 5, 6).reshape(PW, lat_blocks, lon_blocks, WIN, D)

    def split_heads(tensor):
        return tensor.reshape(PW, lat_blocks, lon_blocks, WIN, HEADS, HEAD)

    hidden_win = to_windows(joined)
    grad_win = to_windows(joined_grad)
    projected = jnp.einsum("plnwd,de->plnwe", hidden_win, qkv_weight, precision=HIGH)
    query_heads = split_heads(projected[..., :D])
    key_heads = split_heads(projected[..., D : 2 * D])
    value_heads = split_heads(projected[..., 2 * D :])
    split_table = bias_table.reshape(lat_blocks, PW, HEADS, LONREL, WZ, WZ, WLAT, WLAT)
    bias_full = jnp.einsum("lchrijab,xyr->clhiaxjby", split_table, onehot, precision=HIGH)
    bias_full = bias_full.reshape(PW, lat_blocks, HEADS, WIN, WIN)
    bias_masked = jnp.where(level_valid()[:, None, None], bias_full, -jnp.inf)
    scores = (
        jnp.einsum("plnahe,plnbhe->plnhab", query_heads, key_heads, precision=HIGH) * score_scale
        + bias_masked[:, :, None]
    )
    row_max = jnp.max(scores, axis=-1, keepdims=True)
    exponent = jnp.exp(scores - row_max)
    attention = exponent * (1.0 / jnp.sum(exponent, axis=-1, keepdims=True))
    mixture = jnp.einsum("plnhab,plnbhe->plnahe", attention, value_heads, precision=HIGH).reshape(
        PW, lat_blocks, lon_blocks, WIN, D
    )
    grad_out_w = jnp.einsum("plnwd,plnwe->de", mixture, grad_win, precision=HIGH)
    grad_mixture = split_heads(jnp.einsum("plnwe,de->plnwd", grad_win, out_weight, precision=HIGH))
    grad_attention = jnp.einsum("plnahe,plnbhe->plnhab", grad_mixture, value_heads, precision=HIGH)
    grad_values = jnp.einsum("plnhab,plnahe->plnbhe", attention, grad_mixture, precision=HIGH)
    grad_scores = attention * (
        grad_attention - jnp.sum(attention * grad_attention, axis=-1, keepdims=True)
    )
    grad_queries = (
        jnp.einsum("plnhab,plnbhe->plnahe", grad_scores, key_heads, precision=HIGH) * score_scale
    )
    grad_keys = (
        jnp.einsum("plnhab,plnahe->plnbhe", grad_scores, query_heads, precision=HIGH) * score_scale
    )
    merged_shape = (PW, lat_blocks, lon_blocks, WIN, D)
    grad_projected = jnp.concatenate(
        [
            grad_queries.reshape(merged_shape),
            grad_keys.reshape(merged_shape),
            grad_values.reshape(merged_shape),
        ],
        axis=-1,
    )
    grad_qkv_w = jnp.einsum("plnwd,plnwe->de", hidden_win, grad_projected, precision=HIGH)
    grad_hidden = jnp.einsum("plnwe,de->plnwd", grad_projected, qkv_weight, precision=HIGH)
    score_sum = jnp.sum(grad_scores, axis=2).reshape(
        PW, lat_blocks, HEADS, WZ, WLAT, WLON, WZ, WLAT, WLON
    )
    bias_local = jnp.einsum("clhiaxjby,xyr->lchrijab", score_sum, onehot, precision=HIGH)
    bias_local = bias_local.reshape(lat_blocks, PW, HEADS, LONREL, PAIRS)
    shaped = grad_hidden.reshape(PW, lat_blocks, lon_blocks, WZ, WLAT, WLON, D)
    back_block = shaped.transpose(0, 3, 1, 4, 2, 5, 6).reshape(
        ZP, lat_blocks * WLAT, lon_blocks * WLON, D
    )
    returned = passed_along(back_block[:, :, :half_cols], "lon", -1)
    grad_lifted = jnp.concatenate([back_block[:, :, half_cols:], returned], axis=2)
    grad_normed = jnp.roll(grad_lifted, -1, 0)
    grad_unit = grad_normed * norm_gain
    grad_features = cotangent + inverse * (
        grad_unit
        - jnp.mean(grad_unit, -1, keepdims=True)
        - standard * jnp.mean(grad_unit * standard, -1, keepdims=True)
    )
    token_count = (
        ZP * features.shape[1] * features.shape[2] * lax.axis_size("lat") * lax.axis_size("lon")
    )
    factor = 1.0 / math.sqrt(token_count)
    norm_local = (
        jnp.stack(
            [jnp.sum(grad_normed * standard, axis=(0, 1, 2)), jnp.sum(grad_normed, axis=(0, 1, 2))]
        )
        * factor
    )
    weights_local = jnp.concatenate([grad_qkv_w, grad_out_w], axis=1) * factor
    grad_bias = lax.psum(bias_local, "lon")
    grad_norm = lax.psum(norm_local, ("lat", "lon"))
    column_part = lax.psum_scatter(weights_local, "lon", scatter_dimension=1, tiled=True)
    grad_weights = lax.psum_scatter(column_part, "lat", scatter_dimension=0, tiled=True)
    return (grad_features, grad_weights, grad_bias, grad_norm)


def solution(mesh):
    placed = (
        P(None, "lat", "lon", None),
        P(None, "lat", "lon", None),
        P(),
        P(),
        P(),
        P(),
        P("lat", None, None, None, None),
    )
    return jax.shard_map(
        shards,
        mesh=mesh,
        in_specs=placed,
        out_specs=(
            P(None, "lat", "lon", None),
            P("lat", "lon"),
            P("lat", None, None, None, None),
            P(),
        ),
        check_vma=False,
    )
```

profile of v0, /device:TPU:18, one launch (start us, length us, event | category | flops | bytes accessed | tf_op | source)
XLA Modules:
  0.0 643.1 jit_solution(16595342032488264519)
XLA Ops:
  7.2 1.1 slice.55
  8.3 1.0 fusion.30
  9.4 5.7 collective-permute-start.1
  15.1 1.1 reduce_sum.93
  16.3 1.2 fusion.24
  17.6 1.1 multiply_add_fusion
  18.8 2.7 collective-permute-start
  21.6 0.6 copy.128
  22.2 8.9 %convolution_bitcast_fusion = f32[2,1,6,2,6,12,2,6,12]{8,7,4,6,3,2,0,5,1:T(8,128)} fusion(f32[2,6,23,2,2,6,6]{2,0,6,5,4,3,1:T(2,128)S(1)} %bitcast.106, s32[12,12]{1,0:T(8,128)S(1)} %subtract_add_fusion), kind=kOutput, calls=%fused_computation | convolution fusion | flops 68680944 | bytes 1154880 | tf_op jit(solution)/shard_map/lchrijab,xyr->clhiaxjby/dot_general | solution.py:76
  31.2 20.7 %copy.165 = f32[2,1,6,2,6,12,2,6,12]{5,4,3,8,7,6,2,0,1:T(8,128)} copy(f32[2,1,6,2,6,12,2,6,12]{8,7,4,6,3,2,0,5,1:T(8,128)} %convolution_bitcast_fusion) | data formatting | bytes 1990656 | tf_op jit(solution)/shard_map/reshape | solution.py:77
  51.9 10.3 %reshape.280 = f32[2,6,144,144]{2,3,1,0:T(8,128)} reshape(f32[2,1,6,2,6,12,2,6,12]{5,4,3,8,7,6,2,0,1:T(8,128)} %copy.165) | data formatting | bytes 1990656 | tf_op jit(solution)/shard_map/reshape | solution.py:77
  62.4 0.8 reshape.274
  63.3 0.9 convolution_bitcast_fusion.2
  64.2 0.8 fusion.42
  65.0 0.2 copy.127
  65.2 0.2 copy.126
  65.4 3.4 fusion.44
  68.8 0.3 fusion.2
  69.1 1.1 copy.133
  70.3 1.5 fusion.27
  71.8 2.7 fusion.13
  74.5 2.0 multiply_reduce_fusion
  76.5 0.5 subtract_multiply_fusion
  77.0 2.5 convolution_multiply_fusion
  79.5 1.8 convolution_multiply_fusion.1
  81.3 2.0 fusion.11
  83.4 1.1 reshape.262
  84.5 0.2 copy.147
  84.7 1.4 copy.146
  86.1 0.2 copy.145
  86.2 0.5 convolution_bitcast_fusion.4
  86.8 1.2 convolution_bitcast_fusion.3
  88.1 1.0 maximum_multiply_fusion
  89.0 2.2 copy.168
  91.3 1.3 dynamic-slice.4
  93.2 8.6 %reshape.282 = f32[2,6,2,6,12,2,6,12]{4,3,2,7,6,5,1,0:T(8,128)} reshape(f32[2,6,144,144]{2,3,1,0:T(8,128)S(1)} %copy-done.2) | data formatting | bytes 1990656 | tf_op jit(solution)/shard_map/reshape.58
  101.8 0.5 copy.139
  102.3 0.3 concatenate.41
  102.6 0.2 copy-done.6
  102.8 0.5 copy.137
  103.3 0.3 concatenate.40
  103.6 0.5 copy.135
  104.1 0.3 concatenate.39
  104.4 1.1 fusion.5
  105.5 4.0 collective-permute-start.2
  109.6 20.1 %copy.151 = f32[2,6,2,6,12,2,6,12]{7,6,4,5,3,2,1,0:T(8,128)} copy(f32[2,6,2,6,12,2,6,12]{4,3,2,7,6,5,1,0:T(8,128)} %reshape.282) | data formatting | bytes 1990656 | tf_op jit(solution)/shard_map/reshape.58
  129.7 13.0 %convolution_bitcast_fusion.1 = f32[1,2,6,23,2,2,6,6]{3,7,5,6,4,2,1,0:T(8,128)S(1)} fusion(f32[2,6,2,6,12,2,6,12]{7,6,4,5,3,2,1,0:T(8,128)} %copy.151, s32[12,12]{1,0:T(8,128)S(1)} %subtract_add_fusion), kind=kOutput, calls=%fused_computation.7 | convolution fusion | flops 68680944 | bytes 1154880 | tf_op jit(solution)/shard_map/clhiaxjby,xyr->lchrijab/dot_general | solution.py:116
  142.7 1.6 copy.152
  144.5 0.4 multiply_reduce_fusion.1
  144.9 0.4 copy-done.9
  145.3 0.3 copy_add_fusion
  145.6 172.4 %reduce-scatter.6.cloned.1.call-done = f32[24,192]{1,0:T(8,128)} async-done(((f32[768,192]{1,0:T(8,128)}), f32[24,192]{1,0:T(8,128)}) %reduce-scatter.6.cloned.1.call-update) | async-done | bytes 18448
  317.9 0.8 copy.169
  318.7 26.8 %fusion = f32[16,24]{1,0:T(8,128)S(1)} fusion(f32[192,24]{1,0:T(8,128)S(1)} %copy.169), kind=kCustom, calls=%all-reduce-scatter | all-reduce-scatter fusion | flops 6145 | bytes 22016
  345.5 1.3 collective-permute-start.5
  346.8 5.5 collective-permute-start.4
  352.3 5.2 collective-permute-start.3
  357.6 2.7 collective-permute-start.6
  360.3 0.9 copy.153
  361.2 98.1 %psum.15 = f32[2,192]{1,0:T(2,128)} all-reduce(f32[2,192]{1,0:T(2,128)S(1)} %maximum_multiply_fusion.1), channel_id=1, replica_groups=mesh['lat'=16,'lon'=32] {'lat','lon'}, use_global_device_ids=true, to_apply=%region_13.14 | all-reduce | flops 384 | bytes 3072 | tf_op jit(solution)/shard_map/psum | solution.py:143
  459.3 173.6 %all-reduce.4.cloned.1.call-done = f32[1,2,6,23,144]{3,1,4,2,0:T(2,128)} async-done(((f32[1,2,6,23,144]{3,1,4,2,0:T(2,128)}), f32[1,2,6,23,144]{3,1,4,2,0:T(2,128)}) %all-reduce.4.cloned.1.call-update) | async-done | bytes 158992 | tf_op jit(solution)/shard_map/psum | solution.py:142
  632.9 2.2 copy.154
  635.1 0.5 concatenate.47
  635.6 0.6 constant_dynamic-slice_fusion
  (62 shorter events, 1.1 us)
Async XLA Ops:
  7.2 56.1 %copy-start = (f32[192,576]{1,0:T(8,128)S(1)}, f32[192,576]{1,0:T(8,128)}, u32[]{:S(2)}) copy-start(f32[192,576]{1,0:T(8,128)} %param.11) | copy-start | bytes 1327108
  7.2 310.7 %reduce-scatter.6.cloned.1.call-start = ((), (), s32[]{:S(2)}) async-start(), calls=%async_computation.2 | async-start | bytes 811008
  8.3 13.2 %copy-start.13 = (f32[1,2,6,23,144]{4,1,3,2,0:T(2,128)S(1)}, f32[1,2,6,23,144]{4,1,3,2,0:T(2,128)}, u32[]{:S(2)}) copy-start(f32[1,2,6,23,144]{4,1,3,2,0:T(2,128)} %param.13) | copy-start | bytes 476932
  9.4 52.8 %collective-permute-start.1 = (f32[4,6,6,192]{3,0,2,1:T(4,128)S(1)}, f32[4,6,6,192]{3,0,2,1:T(4,128)S(1)}, u32[]{:S(2)}, u32[]{:S(2)}) collective-permute-start(f32[4,6,6,192]{3,0,2,1:T(4,128)S(1)} %fusion.30), channel_id=1, source_target_pairs={{0,1},{1,2},{2,3},{3,4},{4,5},{5,6},{6,7},{7,8},{8,9},{9,10},{10,1... | collective-permute-start | bytes 331784 | tf_op jit(solution)/shard_map/ppermute | solution.py:25
  18.8 44.4 %collective-permute-start = (f32[4,6,6,192]{3,2,1,0:T(8,128)S(1)}, f32[4,6,6,192]{3,2,1,0:T(8,128)S(1)}, u32[]{:S(2)}, u32[]{:S(2)}) collective-permute-start(f32[4,6,6,192]{3,2,1,0:T(8,128)S(1)} %fusion.29), channel_id=1, source_target_pairs={{0,1},{1,2},{2,3},{3,4},{4,5},{5,6},{6,7},{7,8},{8,9},{9,10},{10,1... | collective-permute-start | bytes 331784 | tf_op jit(solution)/shard_map/ppermute | solution.py:25
  51.9 10.3 %copy-start.8 = (f32[4,6,12,192]{3,0,2,1:T(4,128)S(1)}, f32[4,6,12,192]{3,0,2,1:T(4,128)}, u32[]{:S(2)}) copy-start(f32[4,6,12,192]{3,0,2,1:T(4,128)} %param.8) | copy-start | bytes 663556
  62.4 1.8 copy-start.7
  63.3 1.9 copy-start.10
  77.0 4.3 copy-start.1
  81.3 3.2 copy-start.4
  81.3 4.7 copy-start.5
  83.4 2.9 copy-start.12
  83.4 3.4 copy-start.11
  88.0 5.2 copy-start.2
  91.2 541.6 %all-reduce.4.cloned.1.call-start = ((), (), s32[]{:S(2)}) async-start(), calls=%async_computation.1 | async-start | bytes 1769472 | tf_op jit(solution)/shard_map/psum | solution.py:142
  101.8 1.0 copy-start.6
  105.5 38.8 %collective-permute-start.2 = (f32[4,6,6,192]{3,2,1,0:T(8,128)S(1)}, f32[4,6,6,192]{3,2,1,0:T(8,128)S(1)}, u32[]{:S(2)}, u32[]{:S(2)}) collective-permute-start(f32[4,6,6,192]{3,2,1,0:T(8,128)S(1)} %get-tuple-element.35), channel_id=1, source_target_pairs={{0,31},{1,0},{2,1},{3,2},{4,3},{5,4},{6,5},{7,6},{8,7},{9,8},{10,9... | collective-permute-start | bytes 331784 | tf_op jit(solution)/shard_map/ppermute | solution.py:25
  142.6 1.8 copy-start.3
  142.7 1.8 copy-start.14
  144.3 1.0 copy-start.9
  345.5 289.6 %collective-permute-start.5 = (f32[16,24]{1,0:T(8,128)S(1)}, f32[16,24]{1,0:T(8,128)S(1)}, u32[]{:S(2)}, u32[]{:S(2)}) collective-permute-start(f32[16,24]{1,0:T(8,128)S(1)} %fusion), channel_id=1, source_target_pairs={{0,96},{32,128},{64,160},{96,192},{128,224},{160,256},{192,288},{2... | collective-permute-start | bytes 4616
  346.8 288.3 %collective-permute-start.4 = (f32[16,24]{1,0:T(8,128)S(1)}, f32[16,24]{1,0:T(8,128)S(1)}, u32[]{:S(2)}, u32[]{:S(2)}) collective-permute-start(f32[16,24]{1,0:T(8,128)S(1)} %fusion), channel_id=1, source_target_pairs={{0,64},{32,96},{64,128},{96,160},{128,192},{160,224},{192,256},{22... | collective-permute-start | bytes 4616
  352.3 282.8 %collective-permute-start.3 = (f32[16,24]{1,0:T(8,128)S(1)}, f32[16,24]{1,0:T(8,128)S(1)}, u32[]{:S(2)}, u32[]{:S(2)}) collective-permute-start(f32[16,24]{1,0:T(8,128)S(1)} %fusion), channel_id=1, source_target_pairs={{0,32},{32,64},{64,96},{96,128},{128,160},{160,192},{192,224},{224... | collective-permute-start | bytes 4616
  357.6 277.5 %collective-permute-start.6 = (f32[12,24]{1,0:T(8,128)S(1)}, f32[12,24]{1,0:T(8,128)S(1)}, u32[]{:S(2)}, u32[]{:S(2)}) collective-permute-start(f32[12,24]{1,0:T(8,128)S(1)} %slice.77), channel_id=1, source_target_pairs={{0,128},{32,160},{64,192},{96,224},{128,256},{160,288},{192,320},{... | collective-permute-start | bytes 3464
Sparse Core Ops, SparseCore 0:
  91.4 226.4 reduce-scatter.5
  320.8 312.0 all-reduce.3
where the time goes:
time: 645 us; the launch traced here: 643 us
  waiting for transfers between devices  346 us (54%)
  blocking collectives  125 us (19%)
  local copies, waits for them, and re-layouts  80.6 us (12%)
  matrix products  41.6 us (6%)
  starting transfers between devices  27.3 us (4%)
  between operations  15.3 us (2%)
  other arithmetic  7.51 us (1%)
    psum x1, waiting for transfers between devices, shards(): grad_bias = lax.psum(bias_local, 'lon')  174 us
    unnamed x7, waiting for transfers between devices  172 us
    psum x1, blocking collectives, shards(): grad_norm = lax.psum(norm_local, ('lat', 'lon'))  98.1 us
    reshape x2, local copies, waits for them, and re-layouts, shards(): bias_full = bias_full.reshape(PW, lat_blocks, HEADS, WIN, WIN)  30.9 us
    another operation x4, local copies, waits for them, and re-layouts  30.6 us
    unnamed x1, blocking collectives  26.8 us
    unnamed x5, starting transfers between devices  14.8 us
    dot_general x1, matrix products, shards(): jnp.einsum('clhiaxjby,xyr->lchrijab', score_sum, onehot, precision=HIGH)  13 us
  transfers between devices with their start and end apart: 9, of which 2 were waited for; matrix products, arithmetic and copies ran while one was open for 19% of the time, Pallas kernels for 0%

commit v1 on v0

--- a/solution.py
+++ b/solution.py
@@ -139,7 +139,7 @@
         * factor
     )
     weights_local = jnp.concatenate([grad_qkv_w, grad_out_w], axis=1) * factor
-    grad_bias = lax.psum(bias_local, "lon")
+    grad_bias = jnp.sum(lax.all_gather(bias_local, "lon"), axis=0)
     grad_norm = lax.psum(norm_local, ("lat", "lon"))
     column_part = lax.psum_scatter(weights_local, "lon", scatter_dimension=1, tiled=True)
     grad_weights = lax.psum_scatter(column_part, "lat", scatter_dimension=0, tiled=True)

time: 645 us -> 516 us (0.80)
  the two profiles are of different devices: /device:TPU:18 before, /device:TPU:6 now
where the time goes in v1:
time: 516 us; the launch traced here: 510 us
  waiting for transfers between devices  167 us (32%)
  blocking collectives  148 us (29%)
  local copies, waits for them, and re-layouts  90.4 us (18%)
  matrix products  41.6 us (8%)
  starting transfers between devices  33.1 us (6%)
  between operations  15.6 us (3%)
  other arithmetic  14.2 us (3%)
    unnamed x7, waiting for transfers between devices  160 us
    psum x1, blocking collectives, shards(): grad_norm = lax.psum(norm_local, ('lat', 'lon'))  122 us
    reshape x2, local copies, waits for them, and re-layouts, shards(): bias_full = bias_full.reshape(PW, lat_blocks, HEADS, WIN, WIN)  31.3 us
    another operation x4, local copies, waits for them, and re-layouts  30.6 us
    unnamed x1, blocking collectives  26 us
    ppermute x3, starting transfers between devices, passed_along(): return lax.ppermute(value, axis, pairs)  18.6 us
    unnamed x5, starting transfers between devices  14.4 us
    dot_general x1, matrix products, shards(): jnp.einsum('clhiaxjby,xyr->lchrijab', score_sum, onehot, precision=HIGH)  13 us
  transfers between devices with their start and end apart: 9, of which 2 were waited for; matrix products, arithmetic and copies ran while one was open for 24% of the time, Pallas kernels for 0%

profile of v1, /device:TPU:6, one launch (start us, length us, event | category | flops | bytes accessed | tf_op | source)
XLA Modules:
  0.0 509.8 jit_solution(10405856422669881022)
XLA Ops:
  7.2 1.1 slice.55
  8.3 1.0 fusion.30
  9.4 4.5 collective-permute-start.1
  13.9 1.1 reduce_sum.104
  15.1 1.2 fusion.24
  16.4 1.1 multiply_add_fusion
  17.6 5.7 %collective-permute-start = (f32[4,6,6,192]{3,2,1,0:T(8,128)S(1)}, f32[4,6,6,192]{3,2,1,0:T(8,128)S(1)}, u32[]{:S(2)}, u32[]{:S(2)}) collective-permute-start(f32[4,6,6,192]{3,2,1,0:T(8,128)S(1)} %fusion.29), channel_id=1, source_target_pairs={{0,1},{1,2},{2,3},{3,4},{4,5},{5,6},{6,7},{7,8},{8,9},{9,10},{10,1... | collective-permute-start | bytes 331784 | tf_op jit(solution)/shard_map/ppermute | solution.py:25
  23.4 0.6 copy.131
  24.0 8.9 %convolution_bitcast_fusion = f32[2,1,6,2,6,12,2,6,12]{8,7,4,6,3,2,0,5,1:T(8,128)} fusion(f32[2,6,23,2,2,6,6]{2,0,6,5,4,3,1:T(2,128)S(1)} %bitcast.107, s32[12,12]{1,0:T(8,128)S(1)} %subtract_add_fusion), kind=kOutput, calls=%fused_computation | convolution fusion | flops 68680944 | bytes 1154880 | tf_op jit(solution)/shard_map/lchrijab,xyr->clhiaxjby/dot_general | solution.py:76
  33.0 20.7 %copy.170 = f32[2,1,6,2,6,12,2,6,12]{5,4,3,8,7,6,2,0,1:T(8,128)} copy(f32[2,1,6,2,6,12,2,6,12]{8,7,4,6,3,2,0,5,1:T(8,128)} %convolution_bitcast_fusion) | data formatting | bytes 1990656 | tf_op jit(solution)/shard_map/reshape | solution.py:77
  53.7 10.6 %reshape.277 = f32[2,6,144,144]{2,3,1,0:T(8,128)} reshape(f32[2,1,6,2,6,12,2,6,12]{5,4,3,8,7,6,2,0,1:T(8,128)} %copy.170) | data formatting | bytes 1990656 | tf_op jit(solution)/shard_map/reshape | solution.py:77
  64.5 0.8 reshape.271
  65.5 0.9 convolution_bitcast_fusion.2
  66.4 0.8 fusion.42
  67.2 0.2 copy.130
  67.4 0.2 copy.129
  67.6 3.4 fusion.44
  71.0 0.3 fusion.2
  71.3 1.1 copy.136
  72.4 1.5 fusion.27
  74.0 2.7 fusion.13
  76.7 2.0 multiply_reduce_fusion
  78.7 0.5 subtract_multiply_fusion
  79.2 2.5 convolution_multiply_fusion
  81.7 1.8 convolution_multiply_fusion.1
  83.5 2.0 fusion.11
  85.6 1.1 reshape.260
  86.9 11.2 %copy.149 = f32[2,1,1,144,192]{4,3,0,2,1:T(8,128)S(1)} copy(f32[2,1,1,144,192]{3,4,0,2,1:T(8,128)} %bitcast.119) | data formatting | bytes 442368 | tf_op jit(solution)/shard_map/reshape | solution.py:106
  98.3 0.5 convolution_bitcast_fusion.4
  98.9 1.2 convolution_bitcast_fusion.3
  100.1 1.0 maximum_multiply_fusion
  101.1 2.2 copy.173
  103.4 8.6 %reshape.279 = f32[2,6,2,6,12,2,6,12]{4,3,2,7,6,5,1,0:T(8,128)} reshape(f32[2,6,144,144]{2,3,1,0:T(8,128)S(1)} %copy-done.2) | data formatting | bytes 1990656 | tf_op jit(solution)/shard_map/reshape.57
  112.0 20.1 %copy.154 = f32[2,6,2,6,12,2,6,12]{7,6,4,5,3,2,1,0:T(8,128)} copy(f32[2,6,2,6,12,2,6,12]{4,3,2,7,6,5,1,0:T(8,128)} %reshape.279) | data formatting | bytes 1990656 | tf_op jit(solution)/shard_map/reshape.57
  132.0 13.0 %convolution_bitcast_fusion.1 = f32[1,2,6,23,2,2,6,6]{3,7,5,6,4,2,1,0:T(8,128)S(1)} fusion(f32[2,6,2,6,12,2,6,12]{7,6,4,5,3,2,1,0:T(8,128)} %copy.154, s32[12,12]{1,0:T(8,128)S(1)} %subtract_add_fusion), kind=kOutput, calls=%fused_computation.7 | convolution fusion | flops 68680944 | bytes 1154880 | tf_op jit(solution)/shard_map/clhiaxjby,xyr->lchrijab/dot_general | solution.py:116
  145.0 0.7 copy.155
  145.7 1.3 copy.156
  147.0 0.5 copy.142
  147.5 0.3 concatenate.41
  147.8 0.2 copy-done.6
  148.0 0.5 copy.140
  148.5 0.3 concatenate.40
  148.8 0.5 copy.138
  149.2 0.3 concatenate.39
  149.6 1.1 fusion.5
  150.7 8.4 %collective-permute-start.2 = (f32[4,6,6,192]{3,2,1,0:T(8,128)S(1)}, f32[4,6,6,192]{3,2,1,0:T(8,128)S(1)}, u32[]{:S(2)}, u32[]{:S(2)}) collective-permute-start(f32[4,6,6,192]{3,2,1,0:T(8,128)S(1)} %get-tuple-element.35), channel_id=1, source_target_pairs={{0,31},{1,0},{2,1},{3,2},{4,3},{5,4},{6,5},{7,6},{8,7},{9,8},{10,9... | collective-permute-start | bytes 331784 | tf_op jit(solution)/shard_map/ppermute | solution.py:25
  159.2 1.3 dynamic-slice.4
  161.1 6.8 %collective-permute-done.2 = f32[4,6,6,192]{3,2,1,0:T(8,128)S(1)} collective-permute-done((f32[4,6,6,192]{3,2,1,0:T(8,128)S(1)}, f32[4,6,6,192]{3,2,1,0:T(8,128)S(1)}, u32[]{:S(2)}, u32[]{:S(2)}) %collective-permute-start.2) | collective-permute-done | bytes 110624 | tf_op jit(solution)/shard_map/ppermute | solution.py:25
  168.0 0.4 multiply_reduce_fusion.1
  168.5 0.3 copy_add_fusion
  168.8 159.7 %reduce-scatter.6.cloned.1.call-done = f32[24,192]{1,0:T(8,128)} async-done(((f32[768,192]{1,0:T(8,128)}), f32[24,192]{1,0:T(8,128)}) %reduce-scatter.6.cloned.1.call-update) | async-done | bytes 18448
  328.4 0.8 copy.174
  329.3 26.0 %fusion = f32[16,24]{1,0:T(8,128)S(1)} fusion(f32[192,24]{1,0:T(8,128)S(1)} %copy.174), kind=kCustom, calls=%all-reduce-scatter | all-reduce-scatter fusion | flops 6145 | bytes 22016
  355.3 3.8 collective-permute-start.5
  359.1 6.5 %collective-permute-start.4 = (f32[16,24]{1,0:T(8,128)S(1)}, f32[16,24]{1,0:T(8,128)S(1)}, u32[]{:S(2)}, u32[]{:S(2)}) collective-permute-start(f32[16,24]{1,0:T(8,128)S(1)} %fusion), channel_id=1, source_target_pairs={{0,64},{32,96},{64,128},{96,160},{128,192},{160,224},{192,256},{22... | collective-permute-start | bytes 4616
  365.7 1.9 collective-permute-start.3
  367.6 2.1 collective-permute-start.6
  369.7 0.9 copy.158
  370.6 122.4 %psum.7 = f32[2,192]{1,0:T(2,128)} all-reduce(f32[2,192]{1,0:T(2,128)S(1)} %maximum_multiply_fusion.1), channel_id=1, replica_groups=mesh['lat'=16,'lon'=32] {'lat','lon'}, use_global_device_ids=true, to_apply=%region_13.14 | all-reduce | flops 384 | bytes 3072 | tf_op jit(solution)/shard_map/psum | solution.py:143
  493.1 0.5 concatenate.47
  493.6 0.6 constant_dynamic-slice_fusion
  494.2 6.7 %reduce_sum.110 = f32[2,6,23,144]{3,0,2,1:T(2,128)S(1)} reduce(f32[32,1,2,6,23,144]{5,2,4,3,1,0:T(2,128)} %all-gather.2.cloned.1.call-done, f32[]{:T(128)} %constant.12.clone.1), dimensions={0,1}, to_apply=%region_9.10 | reduce | flops 1232064 | bytes 5246212 | tf_op jit(solution)/shard_map/reduce_sum | solution.py:142
  500.9 0.6 copy.176
  501.5 1.3 copy.159
  (65 shorter events, 1.4 us)
Async XLA Ops:
  7.2 58.3 %copy-start = (f32[192,576]{1,0:T(8,128)S(1)}, f32[192,576]{1,0:T(8,128)}, u32[]{:S(2)}) copy-start(f32[192,576]{1,0:T(8,128)} %param.11) | copy-start | bytes 1327108
  7.2 321.3 %reduce-scatter.6.cloned.1.call-start = ((), (), s32[]{:S(2)}) async-start(), calls=%async_computation.2 | async-start | bytes 811008
  8.3 15.0 %copy-start.13 = (f32[1,2,6,23,144]{4,1,3,2,0:T(2,128)S(1)}, f32[1,2,6,23,144]{4,1,3,2,0:T(2,128)}, u32[]{:S(2)}) copy-start(f32[1,2,6,23,144]{4,1,3,2,0:T(2,128)} %param.13) | copy-start | bytes 476932
  9.4 55.0 %collective-permute-start.1 = (f32[4,6,6,192]{3,0,2,1:T(4,128)S(1)}, f32[4,6,6,192]{3,0,2,1:T(4,128)S(1)}, u32[]{:S(2)}, u32[]{:S(2)}) collective-permute-start(f32[4,6,6,192]{3,0,2,1:T(4,128)S(1)} %fusion.30), channel_id=1, source_target_pairs={{0,1},{1,2},{2,3},{3,4},{4,5},{5,6},{6,7},{7,8},{8,9},{9,10},{10,1... | collective-permute-start | bytes 331784 | tf_op jit(solution)/shard_map/ppermute | solution.py:25
  17.6 47.8 %collective-permute-start = (f32[4,6,6,192]{3,2,1,0:T(8,128)S(1)}, f32[4,6,6,192]{3,2,1,0:T(8,128)S(1)}, u32[]{:S(2)}, u32[]{:S(2)}) collective-permute-start(f32[4,6,6,192]{3,2,1,0:T(8,128)S(1)} %fusion.29), channel_id=1, source_target_pairs={{0,1},{1,2},{2,3},{3,4},{4,5},{5,6},{6,7},{7,8},{8,9},{9,10},{10,1... | collective-permute-start | bytes 331784 | tf_op jit(solution)/shard_map/ppermute | solution.py:25
  53.7 10.7 %copy-start.8 = (f32[4,6,12,192]{3,0,2,1:T(4,128)S(1)}, f32[4,6,12,192]{3,0,2,1:T(4,128)}, u32[]{:S(2)}) copy-start(f32[4,6,12,192]{3,0,2,1:T(4,128)} %param.8) | copy-start | bytes 663556
  64.5 1.8 copy-start.7
  65.5 1.9 copy-start.10
  79.2 4.3 copy-start.1
  83.5 3.2 copy-start.4
  83.5 14.6 %copy-start.5 = (f32[2,6,32,144]{3,2,1,0:T(8,128)S(1)}, f32[2,6,32,144]{3,2,1,0:T(8,128)}, u32[]{:S(2)}) copy-start(f32[2,6,32,144]{3,2,1,0:T(8,128)} %convolution_multiply_fusion.1) | copy-start | bytes 663556
  85.6 12.7 %copy-start.12 = (f32[2,6,32,144]{3,2,1,0:T(8,128)S(1)}, f32[2,6,32,144]{3,2,1,0:T(8,128)}, u32[]{:S(2)}) copy-start(f32[2,6,32,144]{3,2,1,0:T(8,128)} %fusion.11) | copy-start | bytes 663556
  85.6 13.3 %copy-start.11 = (f32[2,144,192]{2,1,0:T(8,128)S(1)}, f32[2,144,192]{2,1,0:T(8,128)}, u32[]{:S(2)}) copy-start(f32[2,144,192]{2,1,0:T(8,128)} %copy-done.10) | copy-start | bytes 663556
  100.1 3.3 copy-start.2
  103.3 390.9 %all-gather.2.cloned.1.call-start = ((), (), s32[]{:S(2)}) async-start(), calls=%async_computation.1 | async-start | bytes 9326592 | tf_op jit(solution)/shard_map/all_gather | solution.py:142
  147.0 1.0 copy-start.6
  149.5 18.5 %copy-start.3 = (f32[4,6,12,192]{3,0,2,1:T(4,128)S(1)}, f32[4,6,12,192]{3,0,2,1:T(4,128)}, u32[]{:S(2)}) copy-start(f32[4,6,12,192]{3,0,2,1:T(4,128)} %param.7) | copy-start | bytes 663556
  149.6 18.5 %copy-start.14 = (f32[192]{0:T(256)S(1)}, f32[192]{0:T(256)}, u32[]{:S(2)}) copy-start(f32[192]{0:T(256)} %param.9) | copy-start | bytes 2308
  150.7 17.8 %copy-start.9 = (f32[4,6,12,192]{3,0,2,1:T(4,128)S(1)}, f32[4,6,12,192]{3,0,2,1:T(4,128)}, u32[]{:S(2)}) copy-start(f32[4,6,12,192]{3,0,2,1:T(4,128)} %param.8) | copy-start | bytes 663556
  150.7 17.1 %collective-permute-start.2 = (f32[4,6,6,192]{3,2,1,0:T(8,128)S(1)}, f32[4,6,6,192]{3,2,1,0:T(8,128)S(1)}, u32[]{:S(2)}, u32[]{:S(2)}) collective-permute-start(f32[4,6,6,192]{3,2,1,0:T(8,128)S(1)} %get-tuple-element.35), channel_id=1, source_target_pairs={{0,31},{1,0},{2,1},{3,2},{4,3},{5,4},{6,5},{7,6},{8,7},{9,8},{10,9... | collective-permute-start | bytes 331784 | tf_op jit(solution)/shard_map/ppermute | solution.py:25
  355.3 137.8 %collective-permute-start.5 = (f32[16,24]{1,0:T(8,128)S(1)}, f32[16,24]{1,0:T(8,128)S(1)}, u32[]{:S(2)}, u32[]{:S(2)}) collective-permute-start(f32[16,24]{1,0:T(8,128)S(1)} %fusion), channel_id=1, source_target_pairs={{0,96},{32,128},{64,160},{96,192},{128,224},{160,256},{192,288},{2... | collective-permute-start | bytes 4616
  359.1 133.9 %collective-permute-start.4 = (f32[16,24]{1,0:T(8,128)S(1)}, f32[16,24]{1,0:T(8,128)S(1)}, u32[]{:S(2)}, u32[]{:S(2)}) collective-permute-start(f32[16,24]{1,0:T(8,128)S(1)} %fusion), channel_id=1, source_target_pairs={{0,64},{32,96},{64,128},{96,160},{128,192},{160,224},{192,256},{22... | collective-permute-start | bytes 4616
  365.7 127.4 %collective-permute-start.3 = (f32[16,24]{1,0:T(8,128)S(1)}, f32[16,24]{1,0:T(8,128)S(1)}, u32[]{:S(2)}, u32[]{:S(2)}) collective-permute-start(f32[16,24]{1,0:T(8,128)S(1)} %fusion), channel_id=1, source_target_pairs={{0,32},{32,64},{64,96},{96,128},{128,160},{160,192},{192,224},{224... | collective-permute-start | bytes 4616
  367.6 125.5 %collective-permute-start.6 = (f32[12,24]{1,0:T(8,128)S(1)}, f32[12,24]{1,0:T(8,128)S(1)}, u32[]{:S(2)}, u32[]{:S(2)}) collective-permute-start(f32[12,24]{1,0:T(8,128)S(1)} %slice.77), channel_id=1, source_target_pairs={{0,128},{32,160},{64,192},{96,224},{128,256},{160,288},{192,320},{... | collective-permute-start | bytes 3464
Sparse Core Ops, SparseCore 0:
  103.4 224.9 reduce-scatter.5
  332.2 142.7 all-gather.1
